TPU v7x, 128 devices: a whole 4x4x4 slice. The times are simulated.
128 devices in a mesh: gx: 16 (over z_hi, y, core), gy: 8 (over z_lo, x).
Axes of the slice: x: 4, y: 4, z: 4 (z_hi: 2, z_lo: 2; z = z_hi * 2 + z_lo), core: 2. Of those that a mesh axis runs over, the one named last changes fastest.
Arguments:
- slide_tokens: bfloat16 [128, 1024, 768], P('gy', 'gx'), may hold values from -9 to 9
- tissue: int32 [128, 1024], P('gy', 'gx'), may hold values 0 or 1
- grad_tokens: bfloat16 [128, 1024, 768], P('gy', 'gx'), may hold values from -6 to 6
- w_qkv: bfloat16 [768, 2304], replicated, may hold values from -1 to 1
- w_out: bfloat16 [768, 768], replicated, may hold values from -0.21875 to 0.21875
Outputs:
- block_out: bfloat16 [128, 1024, 768], P('gy', 'gx')
- grad_in: bfloat16 [128, 1024, 768], P('gy', 'gx')
- grad_wqkv: float32 [768, 2304], replicated
- grad_wout: float32 [768, 768], replicated
All inputs are finite; a program needn't handle non-finite values. No bound on the sum of `tissue` on one device may be relied on, other than what follows from the above.
Results may differ from a plain program's by a relative error of at most 0.013.
Values may be sent and summed in bfloat16 or wider, within the bound.
No kernel may reach another device: no remote copies, remote signals or barrier semaphores. Data moves between devices by JAX's collectives and lax.ppermute only.
A program may use at most 256 MiB of HBM per device.

v0:
```python
import math
import jax
import jax.numpy as jnp
from jax import lax
from jax.sharding import PartitionSpec as P

HEADS = 24
WIN = 8
SHIFT = 4
epsilon = 1e-05


def shifted_2(block, axis, distance):
    devices = range(lax.axis_size(axis))
    route = [((i - distance) % len(devices), i) for i in devices]
    return lax.ppermute(block, axis, route)


def windows(tensor):
    row_count, col_count, feature_dim = tensor.shape
    tensor = tensor.reshape(row_count // WIN, WIN, col_count // WIN, WIN, feature_dim)
    return tensor.transpose(0, 2, 1, 3, 4).reshape(-1, WIN * WIN, feature_dim)


def unwindows(tensor, row_count, col_count):
    feature_dim = tensor.shape[-1]
    tensor = tensor.reshape(row_count // WIN, col_count // WIN, WIN, WIN, feature_dim)
    return tensor.transpose(0, 2, 1, 3, 4).reshape(row_count, col_count, feature_dim)


def split_heads(tensor):
    return tensor.reshape(tensor.shape[0], tensor.shape[1], HEADS, -1)


def attend(qkv_win, keep_win):
    model_dim = qkv_win.shape[-1] // 3
    queries = split_heads(qkv_win[..., :model_dim])
    keys_part = split_heads(qkv_win[..., model_dim : 2 * model_dim])
    values_part = split_heads(qkv_win[..., 2 * model_dim :])
    score_scale = 1.0 / math.sqrt(model_dim // HEADS)
    scores = (
        jnp.einsum("wqhd,wkhd->whqk", queries, keys_part, preferred_element_type=jnp.float32)
        * score_scale
    )
    win_tokens = qkv_win.shape[1]
    itself = jnp.eye(win_tokens, dtype=bool)
    allowed = jnp.logical_or(keep_win[:, None, None, :] > 0.5, itself[None, None])
    scores = jnp.where(allowed, scores, -1e30)
    maximum = jnp.max(scores, -1, keepdims=True)
    exponent = jnp.exp(scores - maximum)
    attn_probs = exponent / jnp.sum(exponent, -1, keepdims=True)
    weights_half = attn_probs.astype(jnp.bfloat16)
    mixed_out = jnp.einsum(
        "whqk,wkhd->wqhd", weights_half, values_part, preferred_element_type=jnp.float32
    ).astype(jnp.bfloat16)
    return (mixed_out.reshape(qkv_win.shape[0], win_tokens, model_dim), attn_probs)


def attend_back(qkv_win, attn_probs, grad_mixed):
    model_dim = qkv_win.shape[-1] // 3
    window_count, win_tokens = (qkv_win.shape[0], qkv_win.shape[1])
    queries = split_heads(qkv_win[..., :model_dim])
    keys_part = split_heads(qkv_win[..., model_dim : 2 * model_dim])
    values_part = split_heads(qkv_win[..., 2 * model_dim :])
    score_scale = 1.0 / math.sqrt(model_dim // HEADS)
    grad_heads = split_heads(grad_mixed)
    grad_prob = jnp.einsum(
        "wqhd,wkhd->whqk", grad_heads, values_part, preferred_element_type=jnp.float32
    )
    weights_half = attn_probs.astype(jnp.bfloat16)
    grad_value = jnp.einsum(
        "whqk,wqhd->wkhd", weights_half, grad_heads, preferred_element_type=jnp.float32
    ).astype(jnp.bfloat16)
    grad_score = (
        attn_probs * (grad_prob - jnp.sum(grad_prob * attn_probs, -1, keepdims=True)) * score_scale
    )
    score_half = grad_score.astype(jnp.bfloat16)
    grad_query = jnp.einsum(
        "whqk,wkhd->wqhd", score_half, keys_part, preferred_element_type=jnp.float32
    ).astype(jnp.bfloat16)
    grad_key = jnp.einsum(
        "whqk,wqhd->wkhd", score_half, queries, preferred_element_type=jnp.float32
    ).astype(jnp.bfloat16)
    shape_out = (window_count, win_tokens, model_dim)
    return jnp.concatenate(
        [grad_query.reshape(shape_out), grad_key.reshape(shape_out), grad_value.reshape(shape_out)],
        -1,
    )


def layer_region(shifted, keep_mask, grad_shift, owned_mask, w_qkv, w_out):
    row_count, col_count, model_dim = shifted.shape
    flat_in = shifted.reshape(-1, model_dim).astype(jnp.float32)
    centered = flat_in - jnp.mean(flat_in, -1, keepdims=True)
    inv_sigma = lax.rsqrt(jnp.mean(centered * centered, -1, keepdims=True) + epsilon)
    normed = centered * inv_sigma
    hidden = normed.astype(jnp.bfloat16)
    qkv = jnp.dot(hidden, w_qkv, preferred_element_type=jnp.float32).astype(jnp.bfloat16)
    qkv_win = windows(qkv.reshape(row_count, col_count, -1))
    keep_win = windows(keep_mask[..., None])[..., 0]
    mixed_out, attn_probs = attend(qkv_win, keep_win)
    mixed_flat = unwindows(mixed_out, row_count, col_count).reshape(-1, model_dim)
    output = jnp.dot(mixed_flat, w_out, preferred_element_type=jnp.float32).astype(jnp.bfloat16)
    grad_flat = grad_shift.reshape(-1, model_dim)
    grad_mixed = jnp.dot(grad_flat, w_out.T, preferred_element_type=jnp.float32).astype(
        jnp.bfloat16
    )
    grad_qkv = attend_back(
        qkv_win, attn_probs, windows(grad_mixed.reshape(row_count, col_count, model_dim))
    )
    grad_qkv = unwindows(grad_qkv, row_count, col_count).reshape(-1, 3 * model_dim)
    own_column = owned_mask.reshape(-1, 1).astype(jnp.bfloat16)
    contract = (((0,), (0,)), ((), ()))
    grad_wout = lax.dot_general(
        mixed_flat * own_column, grad_flat, contract, preferred_element_type=jnp.float32
    )
    grad_wqkv = lax.dot_general(
        hidden * own_column, grad_qkv, contract, preferred_element_type=jnp.float32
    )
    grad_hidden = jnp.dot(grad_qkv, w_qkv.T, preferred_element_type=jnp.float32)
    grad_shifted = inv_sigma * (
        grad_hidden
        - jnp.mean(grad_hidden, -1, keepdims=True)
        - normed * jnp.mean(grad_hidden * normed, -1, keepdims=True)
    )
    shape_out = (row_count, col_count, model_dim)
    return (
        output.reshape(shape_out),
        grad_shifted.astype(jnp.bfloat16).reshape(shape_out),
        grad_wqkv,
        grad_wout,
    )


def local(slide_tokens, tissue, grad_tokens, w_qkv, w_out):
    row_count, col_count, model_dim = slide_tokens.shape
    keep_mask = tissue.astype(jnp.bfloat16)
    from_below = shifted_2((slide_tokens[:SHIFT], keep_mask[:SHIFT], grad_tokens[:SHIFT]), "gy", -1)
    tall_x = jnp.concatenate([slide_tokens[SHIFT:], from_below[0]], 0)
    tall_k = jnp.concatenate([keep_mask[SHIFT:], from_below[1]], 0)
    tall_g = jnp.concatenate([grad_tokens[SHIFT:], from_below[2]], 0)
    from_right = shifted_2((tall_x[:, :SHIFT], tall_k[:, :SHIFT], tall_g[:, :SHIFT]), "gx", -1)
    shifted_x = jnp.concatenate([tall_x[:, SHIFT:], from_right[0]], 1)
    shifted_k = jnp.concatenate([tall_k[:, SHIFT:], from_right[1]], 1)
    shifted_g = jnp.concatenate([tall_g[:, SHIFT:], from_right[2]], 1)
    owned_mask = jnp.ones((row_count, col_count), jnp.float32)
    attn_shift, grad_shift, part_qkv, part_out = layer_region(
        shifted_x, shifted_k, shifted_g, owned_mask, w_qkv, w_out
    )
    edge = col_count - SHIFT
    from_left = shifted_2((attn_shift[:, edge:], grad_shift[:, edge:]), "gx", 1)
    wide_attn = jnp.concatenate([from_left[0], attn_shift[:, :edge]], 1)
    wide_grad = jnp.concatenate([from_left[1], grad_shift[:, :edge]], 1)
    bottom = row_count - SHIFT
    from_above = shifted_2((wide_attn[bottom:], wide_grad[bottom:]), "gy", 1)
    attn_tile = jnp.concatenate([from_above[0], wide_attn[:bottom]], 0)
    grad_tile = jnp.concatenate([from_above[1], wide_grad[:bottom]], 0)
    grad_wqkv, grad_wout = lax.psum((part_qkv, part_out), ("gx", "gy"))
    block_out = (slide_tokens.astype(jnp.float32) + attn_tile.astype(jnp.float32)).astype(
        jnp.bfloat16
    )
    grad_in = (grad_tokens.astype(jnp.float32) + grad_tile.astype(jnp.float32)).astype(jnp.bfloat16)
    return (block_out, grad_in, grad_wqkv, grad_wout)


def solution(mesh):
    placed = (P("gy", "gx", None), P("gy", "gx"), P("gy", "gx", None), P(), P())
    return jax.shard_map(
        local,
        mesh=mesh,
        in_specs=placed,
        out_specs=(P("gy", "gx", None), P("gy", "gx", None), P(), P()),
        check_vma=False,
    )
```

profile of v0, /device:TPU:1, one launch (start us, length us, event | category | flops | bytes accessed | tf_op | source)
XLA Modules:
  0.0 433.7 jit_solution(9250790033228147858)
XLA Ops:
  7.2 0.9 convert_element_type.101
  8.1 4.7 %collective-permute-start.2 = (bf16[4,64]{1,0:T(4,128)(2,1)S(1)}, bf16[4,64]{1,0:T(4,128)(2,1)S(1)}, u32[]{:S(2)}, u32[]{:S(2)}) collective-permute-start(bf16[4,64]{1,0:T(4,128)(2,1)S(1)} %slice.99), channel_id=1, source_target_pairs={{1,0},{2,1},{3,2},{4,3},{5,4},{6,5},{7,6},{0,7},{9,8},{10,9},{11,1... | collective-permute-start | bytes 1544 | tf_op jit(solution)/shard_map/ppermute | solution.py:16
  12.8 1.8 slice.88
  15.2 1.8 slice.73
  17.8 2.4 slice.72
  20.2 1.1 slice.87
  21.3 1.5 collective-permute-start.3
  22.9 2.8 collective-permute-done.3
  25.7 0.7 maximum_compare_fusion
  26.4 0.8 gt.22
  27.8 0.8 gt.24
  28.6 1.6 broadcast_or_fusion
  30.3 2.7 collective-permute-done
  32.9 1.0 pad_maximum_fusion.7
  33.9 1.9 collective-permute-start.1
  35.8 1.6 pad_maximum_fusion.6
  37.5 4.3 collective-permute-start.7
  41.7 1.4 slice_maximum_fusion.1
  43.2 2.8 slice_maximum_fusion
  47.3 0.7 div.23
  48.6 1.7 pad_maximum_fusion.3
  50.3 1.2 copy-done.18
  51.5 1.4 convolution_convert_fusion.1
  53.0 1.3 copy.38
  55.5 4.5 %convolution_convert_fusion = bf16[1024,2304]{1,0:T(8,128)(2,1)S(1)} fusion(bf16[1024,768]{1,0:T(8,128)(2,1)S(1)} %fusion.20, bf16[768,2304]{1,0:T(8,128)(2,1)S(1)} %copy-done), kind=kOutput, calls=%fused_computation.12 | convolution fusion | flops 3626237952 | bytes 9830400 | tf_op jit(solution)/shard_map/dot_general | solution.py:98
  60.5 2.3 fusion.40
  62.8 4.1 copy.18
  66.9 4.2 copy.17
  71.1 4.2 copy.15
  75.3 8.2 %reshape_reshape.22 = bf16[16,64,24,32]{3,2,1,0:T(8,128)(2,1)} reshape(bf16[2,8,8,8,768]{4,3,2,1,0:T(8,128)(2,1)} %bitcast.88) | data formatting | bytes 3145728 | tf_op jit(solution)/shard_map/reshape;reshape | solution.py:32
  83.5 7.0 %copy.23 = bf16[16,64,24,32]{1,3,2,0:T(8,128)(2,1)} copy(bf16[16,64,24,32]{3,2,1,0:T(8,128)(2,1)} %reshape_reshape.22) | data formatting | bytes 3145728 | tf_op jit(solution)/shard_map/reshape;reshape | solution.py:32
  90.5 9.2 %fusion.42 = f32[16,24,64,64]{2,3,1,0:T(8,128)} fusion(bf16[16,64,24,32]{1,3,2,0:T(8,128)(2,1)} %copy.23, bf16[16,64,24,32]{1,3,2,0:T(8,128)(2,1)} %bitcast.83), kind=kOutput, calls=%fused_computation.69 | convolution fusion | flops 100663296 | bytes 9437184 | tf_op jit(solution)/shard_map/wqhd,wkhd->whqk/dot_general | solution.py:67
  99.7 10.5 %fusion.41 = (f32[16,24,64]{2,1,0:T(8,128)}, f32[16,24,64,64]{2,3,1,0:T(8,128)}) fusion(pred[16,64,64]{1,2,0:T(8,128)(4,1)} %broadcast_or_fusion, bf16[16,64,24,32]{1,3,2,0:T(8,128)(2,1)} %bitcast.95, bf16[16,64,24,32]{1,3,2,0:T(8,128)(2,1)} %bitcast.93), kind=kOutput, calls=%fused_computation.68 | convolution fusion | flops 106954816 | bytes 9601024 | tf_op jit(solution)/shard_map/sub | solution.py:50
  110.2 19.8 %convert_bitcast_fusion.2 = bf16[16,64,24,32]{1,3,2,0:T(8,128)(2,1)} fusion(bf16[16,64,24,32]{1,3,2,0:T(8,128)(2,1)} %bitcast.94, f32[16,24,64,64]{2,3,1,0:T(8,128)} %fusion.42, f32[16,24,64,64]{2,3,1,0:T(8,128)} %get-tuple-element.12, f32[16,24,64]{2,1,0:T(8,128)} %get-tuple-element.11), kind=kOutput, calls=%fused_computation.24 | convolution fusion | flops 112484416 | bytes 15826944 | tf_op jit(solution)/shard_map/whqk,wkhd->wqhd/dot_general | solution.py:78
  130.0 20.0 %convert_bitcast_fusion.1 = bf16[16,64,24,32]{1,3,2,0:T(8,128)(2,1)} fusion(bf16[16,64,24,32]{1,3,2,0:T(8,128)(2,1)} %bitcast.96, f32[16,24,64,64]{2,3,1,0:T(8,128)} %fusion.42, f32[16,24,64,64]{2,3,1,0:T(8,128)} %get-tuple-element.12, f32[16,24,64]{2,1,0:T(8,128)} %get-tuple-element.11), kind=kOutput, calls=%fused_computation.23 | convolution fusion | flops 112484416 | bytes 15826944 | tf_op jit(solution)/shard_map/whqk,wqhd->wkhd/dot_general | solution.py:81
  150.0 10.7 %convert_bitcast_fusion = bf16[16,64,24,32]{1,3,2,0:T(8,128)(2,1)} fusion(bf16[16,64,24,32]{1,3,2,0:T(8,128)(2,1)} %copy.23, f32[16,24,64,64]{2,3,1,0:T(8,128)} %get-tuple-element.12, f32[16,24,64]{2,1,0:T(8,128)} %get-tuple-element.11), kind=kOutput, calls=%fused_computation.22 | convolution fusion | flops 104595456 | bytes 9535488 | tf_op jit(solution)/shard_map/whqk,wqhd->wkhd/dot_general | solution.py:71
  160.8 8.1 %convert_bitcast_fusion.3 = bf16[16,64,24,32]{1,3,2,0:T(8,128)(2,1)} fusion(bf16[16,64,24,32]{1,3,2,0:T(8,128)(2,1)S(1)} %bitcast.84, f32[16,24,64,64]{2,3,1,0:T(8,128)} %get-tuple-element.12, f32[16,24,64]{2,1,0:T(8,128)S(1)} %copy-done.26), kind=kOutput, calls=%fused_computation.26 | convolution fusion | flops 104595456 | bytes 9535488 | tf_op jit(solution)/shard_map/whqk,wkhd->wqhd/dot_general | solution.py:53
  168.9 6.9 %copy.20 = bf16[16,64,24,32]{3,2,1,0:T(8,128)(2,1)} copy(bf16[16,64,24,32]{1,3,2,0:T(8,128)(2,1)} %convert_bitcast_fusion.3) | data formatting | bytes 3145728 | tf_op jit(solution)/shard_map/convert_element_type | solution.py:55
  175.8 8.2 %reshape_reshape.19 = bf16[2,8,8,8,768]{4,3,2,1,0:T(8,128)(2,1)} reshape(bf16[16,64,24,32]{3,2,1,0:T(8,128)(2,1)} %copy.20) | data formatting | bytes 3145728 | tf_op jit(solution)/shard_map/reshape;reshape | solution.py:27
  184.1 1.7 copy.21
  185.8 1.1 copy-done.20
  186.9 2.9 fusion.44
  189.8 6.9 %copy.30 = bf16[16,64,24,32]{3,2,1,0:T(8,128)(2,1)} copy(bf16[16,64,24,32]{1,3,2,0:T(8,128)(2,1)} %convert_bitcast_fusion) | data formatting | bytes 3145728 | tf_op jit(solution)/shard_map/convert_element_type | solution.py:73
  196.7 8.2 %concatenate.50 = bf16[2,8,8,8,768]{4,3,2,1,0:T(8,128)(2,1)} reshape(bf16[16,64,24,32]{3,2,1,0:T(8,128)(2,1)} %copy.30) | data formatting | bytes 3145728 | tf_op jit(solution)/shard_map/concatenate | solution.py:85
  204.9 6.9 %copy.27 = bf16[16,64,24,32]{3,2,1,0:T(8,128)(2,1)} copy(bf16[16,64,24,32]{1,3,2,0:T(8,128)(2,1)} %convert_bitcast_fusion.1) | data formatting | bytes 3145728 | tf_op jit(solution)/shard_map/convert_element_type | solution.py:83
  211.8 8.2 %concatenate.49 = bf16[2,8,8,8,768]{4,3,2,1,0:T(8,128)(2,1)} reshape(bf16[16,64,24,32]{3,2,1,0:T(8,128)(2,1)} %copy.27) | data formatting | bytes 3145728 | tf_op jit(solution)/shard_map/concatenate | solution.py:85
  220.0 6.9 %copy.25 = bf16[16,64,24,32]{3,2,1,0:T(8,128)(2,1)} copy(bf16[16,64,24,32]{1,3,2,0:T(8,128)(2,1)} %convert_bitcast_fusion.2) | data formatting | bytes 3145728 | tf_op jit(solution)/shard_map/convert_element_type | solution.py:80
  226.9 8.2 %concatenate.48 = bf16[2,8,8,8,768]{4,3,2,1,0:T(8,128)(2,1)} reshape(bf16[16,64,24,32]{3,2,1,0:T(8,128)(2,1)} %copy.25) | data formatting | bytes 3145728 | tf_op jit(solution)/shard_map/concatenate | solution.py:85
  235.1 2.5 maximum_bitcast_fusion
  238.2 0.9 copy-done.3
  239.6 1.7 copy-done.11
  241.2 6.2 %fusion.43 = f32[768,2304]{1,0:T(8,128)} fusion(bf16[1024,768]{1,0:T(8,128)(2,1)S(1)} %bitcast.101, bf16[1024,2304]{1,0:T(8,128)(2,1)S(1)} %bitcast.90), kind=kOutput, calls=%fused_computation.70 | convolution fusion | flops 3623878656 | bytes 13369344 | tf_op jit(solution)/shard_map/dot_general | solution.py:117
  247.5 3.3 convolution_convert_fusion.2
  251.1 4.1 fusion.39
  255.4 0.9 collective-permute-start.5
  256.3 1.1 multiply_convert_fusion.2
  257.5 6.1 %collective-permute-done.8 = bf16[16,4,768]{2,1,0:T(4,128)(2,1)S(1)} collective-permute-done((bf16[16,4,768]{2,1,0:T(4,128)(2,1)S(1)}, bf16[16,4,768]{2,1,0:T(4,128)(2,1)S(1)}, u32[]{:S(2)}, u32[]{:S(2)}) %collective-permute-start.8) | collective-permute-done | bytes 98336 | tf_op jit(solution)/shard_map/ppermute | solution.py:16
  263.8 3.3 collective-permute-done.5
  267.1 1.9 add_convert_fusion.1
  269.0 12.7 %collective-permute-done.9 = bf16[4,64,768]{2,1,0:T(8,128)(2,1)S(1)} collective-permute-done((bf16[4,64,768]{2,1,0:T(8,128)(2,1)S(1)}, bf16[4,64,768]{2,1,0:T(8,128)(2,1)S(1)}, u32[]{:S(2)}, u32[]{:S(2)}) %collective-permute-start.9) | collective-permute-done | bytes 393248 | tf_op jit(solution)/shard_map/ppermute | solution.py:16
  281.6 1.8 add_convert_fusion
  283.5 135.1 %all-reduce.3.cloned.1.call-done = (f32[768,2304]{1,0:T(8,128)}, f32[768,768]{1,0:T(8,128)}) async-done(((f32[768,2304]{1,0:T(8,128)}, f32[768,768]{1,0:T(8,128)}), (f32[768,2304]{1,0:T(8,128)}, f32[768,768]{1,0:T(8,128)})) %all-reduce.3.cloned.1.call-update) | async-done | bytes 9437200 | tf_op jit(solution)/shard_map/psum | solution.py:158
  418.6 6.6 %copy.42 = f32[768,2304]{1,0:T(8,128)} copy(f32[768,2304]{1,0:T(8,128)} %get-tuple-element.18) | data formatting | bytes 14155776
  425.2 1.4 copy.43
  (82 shorter events, 7.6 us)
Async XLA Ops:
  7.2 48.3 %copy-start = (bf16[768,2304]{1,0:T(8,128)(2,1)S(1)}, bf16[768,2304]{1,0:T(8,128)(2,1)}, u32[]{:S(2)}) copy-start(bf16[768,2304]{1,0:T(8,128)(2,1)} %param.8) | copy-start | bytes 10616836
  7.2 411.4 %all-reduce.3.cloned.1.call-start = ((), (), s32[]{:S(2)}) async-start(), calls=%async_computation | async-start | bytes 18874368 | tf_op jit(solution)/shard_map/psum | solution.py:158
  7.2 13.0 %copy-start.9 = (bf16[16,64,768]{2,1,0:T(8,128)(2,1)S(1)}, bf16[16,64,768]{2,1,0:T(8,128)(2,1)}, u32[]{:S(2)}) copy-start(bf16[16,64,768]{2,1,0:T(8,128)(2,1)} %param.7) | copy-start | bytes 4718596
  8.1 13.2 %collective-permute-start.2 = (bf16[4,64]{1,0:T(4,128)(2,1)S(1)}, bf16[4,64]{1,0:T(4,128)(2,1)S(1)}, u32[]{:S(2)}, u32[]{:S(2)}) collective-permute-start(bf16[4,64]{1,0:T(4,128)(2,1)S(1)} %slice.99), channel_id=1, source_target_pairs={{1,0},{2,1},{3,2},{4,3},{5,4},{6,5},{7,6},{0,7},{9,8},{10,9},{11,1... | collective-permute-start | bytes 1544 | tf_op jit(solution)/shard_map/ppermute | solution.py:16
  14.5 21.3 %collective-permute-start.6 = (bf16[4,64,768]{2,1,0:T(8,128)(2,1)}, bf16[4,64,768]{2,1,0:T(8,128)(2,1)}, u32[]{:S(2)}, u32[]{:S(2)}) collective-permute-start(bf16[4,64,768]{2,1,0:T(8,128)(2,1)} %slice.88), channel_id=1, source_target_pairs={{1,0},{2,1},{3,2},{4,3},{5,4},{6,5},{7,6},{0,7},{9,8},{10,9},{11,1... | collective-permute-start | bytes 1179656 | tf_op jit(solution)/shard_map/ppermute | solution.py:16
  16.9 16.0 %collective-permute-start = (bf16[4,64,768]{2,1,0:T(8,128)(2,1)}, bf16[4,64,768]{2,1,0:T(8,128)(2,1)}, u32[]{:S(2)}, u32[]{:S(2)}) collective-permute-start(bf16[4,64,768]{2,1,0:T(8,128)(2,1)} %slice.73), channel_id=1, source_target_pairs={{1,0},{2,1},{3,2},{4,3},{5,4},{6,5},{7,6},{0,7},{9,8},{10,9},{11,1... | collective-permute-start | bytes 1179656 | tf_op jit(solution)/shard_map/ppermute | solution.py:16
  21.3 4.4 %collective-permute-start.3 = (bf16[16,4]{1,0:T(8,128)(2,1)S(1)}, bf16[16,4]{1,0:T(8,128)(2,1)S(1)}, u32[]{:S(2)}, u32[]{:S(2)}) collective-permute-start(bf16[16,4]{1,0:T(8,128)(2,1)S(1)} %pad_maximum_fusion.8), channel_id=1, source_target_pairs={{8,0},{16,8},{24,16},{32,24},{40,32},{48,40},{56,48},{64,56},{72,6... | collective-permute-start | bytes 392 | tf_op jit(solution)/shard_map/ppermute | solution.py:16
  28.6 13.1 %copy-start.7 = (bf16[12,64,768]{2,1,0:T(8,128)(2,1)S(1)}, bf16[12,64,768]{2,1,0:T(8,128)(2,1)}, u32[]{:S(2)}) copy-start(bf16[12,64,768]{2,1,0:T(8,128)(2,1)} %slice.72) | copy-start | bytes 3538948
  30.2 12.9 %copy-start.6 = (bf16[12,64,768]{2,1,0:T(8,128)(2,1)S(1)}, bf16[12,64,768]{2,1,0:T(8,128)(2,1)}, u32[]{:S(2)}) copy-start(bf16[12,64,768]{2,1,0:T(8,128)(2,1)} %slice.87) | copy-start | bytes 3538948
  33.9 12.1 %collective-permute-start.1 = (bf16[16,4,768]{2,1,0:T(4,128)(2,1)S(1)}, bf16[16,4,768]{2,1,0:T(4,128)(2,1)S(1)}, u32[]{:S(2)}, u32[]{:S(2)}) collective-permute-start(bf16[16,4,768]{2,1,0:T(4,128)(2,1)S(1)} %pad_maximum_fusion.7), channel_id=1, source_target_pairs={{8,0},{16,8},{24,16},{32,24},{40,32},{48,40},{56,48},{64,56},{72,6... | collective-permute-start | bytes 294920 | tf_op jit(solution)/shard_map/ppermute | solution.py:16
  37.5 11.2 %collective-permute-start.7 = (bf16[16,4,768]{2,1,0:T(4,128)(2,1)}, bf16[16,4,768]{2,1,0:T(4,128)(2,1)}, u32[]{:S(2)}, u32[]{:S(2)}) collective-permute-start(bf16[16,4,768]{2,1,0:T(4,128)(2,1)} %pad_maximum_fusion.6), channel_id=1, source_target_pairs={{8,0},{16,8},{24,16},{32,24},{40,32},{48,40},{56,48},{64,56},{72,6... | collective-permute-start | bytes 294920 | tf_op jit(solution)/shard_map/ppermute | solution.py:16
  43.2 4.1 copy-start.1
  46.0 0.6 copy-start.13
  48.6 2.9 copy-start.25
  50.3 1.2 copy-start.18
  53.0 2.0 copy-start.2
  53.0 2.0 copy-start.14
  53.0 2.0 copy-start.21
  53.0 2.0 copy-start.23
  150.0 10.8 %copy-start.5 = (bf16[16,64,768]{1,2,0:T(8,128)(2,1)S(1)}, bf16[16,64,768]{1,2,0:T(8,128)(2,1)}, u32[]{:S(2)}) copy-start(bf16[16,64,768]{1,2,0:T(8,128)(2,1)} %copy.15) | copy-start | bytes 4718596
  150.0 10.8 %copy-start.26 = (f32[16,24,64]{2,1,0:T(8,128)S(1)}, f32[16,24,64]{2,1,0:T(8,128)}, u32[]{:S(2)}) copy-start(f32[16,24,64]{2,1,0:T(8,128)} %get-tuple-element.11) | copy-start | bytes 294916
  184.1 2.8 copy-start.19
  185.7 1.1 copy-start.20
  237.7 1.4 copy-start.3
  237.7 1.4 copy-start.15
  239.1 2.2 copy-start.11
  247.5 3.5 copy-start.4
  247.5 3.6 copy-start.12
  247.5 3.6 copy-start.16
  247.5 3.6 copy-start.22
  247.5 3.6 copy-start.24
  250.9 4.4 %collective-permute-start.4 = (bf16[16,4,768]{2,1,0:T(4,128)(2,1)S(1)}, bf16[16,4,768]{2,1,0:T(4,128)(2,1)S(1)}, u32[]{:S(2)}, u32[]{:S(2)}) collective-permute-start(bf16[16,4,768]{2,1,0:T(4,128)(2,1)S(1)} %slice.104), channel_id=1, source_target_pairs={{120,0},{0,8},{8,16},{16,24},{24,32},{32,40},{40,48},{48,56},{56,6... | collective-permute-start | bytes 294920 | tf_op jit(solution)/shard_map/ppermute | solution.py:16
  255.4 11.7 %collective-permute-start.5 = (bf16[4,64,768]{2,1,0:T(8,128)(2,1)S(1)}, bf16[4,64,768]{2,1,0:T(8,128)(2,1)S(1)}, u32[]{:S(2)}, u32[]{:S(2)}) collective-permute-start(bf16[4,64,768]{2,1,0:T(8,128)(2,1)S(1)} %pad_maximum_fusion.5), channel_id=1, source_target_pairs={{7,0},{0,1},{1,2},{2,3},{3,4},{4,5},{5,6},{6,7},{15,8},{8,9},{9,10... | collective-permute-start | bytes 1179656 | tf_op jit(solution)/shard_map/ppermute | solution.py:16
  256.3 10.8 %copy-start.8 = (bf16[16,64,768]{2,1,0:T(8,128)(2,1)S(1)}, bf16[16,64,768]{2,1,0:T(8,128)(2,1)}, u32[]{:S(2)}) copy-start(bf16[16,64,768]{2,1,0:T(8,128)(2,1)} %param.5) | copy-start | bytes 4718596
  257.4 6.2 %collective-permute-start.8 = (bf16[16,4,768]{2,1,0:T(4,128)(2,1)S(1)}, bf16[16,4,768]{2,1,0:T(4,128)(2,1)S(1)}, u32[]{:S(2)}, u32[]{:S(2)}) collective-permute-start(bf16[16,4,768]{2,1,0:T(4,128)(2,1)S(1)} %slice.108), channel_id=1, source_target_pairs={{120,0},{0,8},{8,16},{16,24},{24,32},{32,40},{40,48},{48,56},{56,6... | collective-permute-start | bytes 294920 | tf_op jit(solution)/shard_map/ppermute | solution.py:16
  263.6 18.0 %copy-start.10 = (bf16[16,64,768]{2,1,0:T(8,128)(2,1)S(1)}, bf16[16,64,768]{2,1,0:T(8,128)(2,1)}, u32[]{:S(2)}) copy-start(bf16[16,64,768]{2,1,0:T(8,128)(2,1)} %param.7) | copy-start | bytes 4718596
  263.8 17.9 %collective-permute-start.9 = (bf16[4,64,768]{2,1,0:T(8,128)(2,1)S(1)}, bf16[4,64,768]{2,1,0:T(8,128)(2,1)S(1)}, u32[]{:S(2)}, u32[]{:S(2)}) collective-permute-start(bf16[4,64,768]{2,1,0:T(8,128)(2,1)S(1)} %pad_maximum_fusion.4), channel_id=1, source_target_pairs={{7,0},{0,1},{1,2},{2,3},{3,4},{4,5},{5,6},{6,7},{15,8},{8,9},{9,10... | collective-permute-start | bytes 1179656 | tf_op jit(solution)/shard_map/ppermute | solution.py:16
  418.6 6.6 %copy-start.17 = (f32[768,768]{1,0:T(8,128)S(1)}, f32[768,768]{1,0:T(8,128)}, u32[]{:S(2)}) copy-start(f32[768,768]{1,0:T(8,128)} %get-tuple-element.19) | copy-start | bytes 7077892
Sparse Core Ops, SparseCore 0:
  247.6 170.9 all-reduce.2
where the time goes:
time: 441 us; the launch traced here: 434 us
  waiting for transfers between devices  163 us (37%)
  local copies, waits for them, and re-layouts  119 us (27%)
  matrix products  101 us (23%)
  other arithmetic  21.9 us (5%)
  between operations  14.7 us (3%)
  starting transfers between devices  14.5 us (3%)
    psum x1, waiting for transfers between devices, local(): grad_wqkv, grad_wout = lax.psum((part_qkv, part_out), ('gx', 'gy'))  135 us
    ppermute x10, waiting for transfers between devices, shifted_2(): return lax.ppermute(block, axis, route)  27.6 us
    concatenate x3, local copies, waits for them, and re-layouts, attend_back(): jnp.concatenate([grad_query.reshape(shape_out), grad_key.reshape(shape_ou...  24.6 us
    dot_general x1, matrix products, attend_back(): jnp.einsum('whqk,wqhd->wkhd', score_half, queries, preferred_element_type...  20 us
    dot_general x1, matrix products, attend_back(): jnp.einsum('whqk,wkhd->wqhd', score_half, keys_part, preferred_element_ty...  19.8 us
    another operation x2, local copies, waits for them, and re-layouts, split_heads(): return tensor.reshape(tensor.shape[0], tensor.shape[1], HEADS, -1)  15.2 us
    ppermute x10, starting transfers between devices, shifted_2(): return lax.ppermute(block, axis, route)  14.5 us
    unnamed x56, local copies, waits for them, and re-layouts  14 us
  transfers between devices with their start and end apart: 11, of which 6 were waited for; matrix products, arithmetic and copies ran while one was open for 8% of the time, Pallas kernels for 0%

commit v1 on v0

--- a/solution.py
+++ b/solution.py
@@ -155,7 +155,10 @@
     from_above = shifted_2((wide_attn[bottom:], wide_grad[bottom:]), "gy", 1)
     attn_tile = jnp.concatenate([from_above[0], wide_attn[:bottom]], 0)
     grad_tile = jnp.concatenate([from_above[1], wide_grad[:bottom]], 0)
-    grad_wqkv, grad_wout = lax.psum((part_qkv, part_out), ("gx", "gy"))
+    run_boxes_by_axis = lambda array_here, net_axis, axis_key: lax.psum(
+        lax.psum(array_here, axis_name=net_axis), axis_key
+    )
+    grad_wqkv, grad_wout = run_boxes_by_axis((part_qkv, part_out), "gy", "gx")
     block_out = (slide_tokens.astype(jnp.float32) + attn_tile.astype(jnp.float32)).astype(
         jnp.bfloat16
     )

time: 441 us -> 648 us (1.47)
  waiting for transfers between devices: 163 us -> 365 us
    psum x1 -> x2, waiting for transfers between devices: 135 us -> 330 us  [the longest x1 202 us: local(): lax.psum(array_here, axis_name=net_axis)]
    ppermute x10, waiting for transfers between devices: 27.6 us -> 35.3 us  [shifted_2(): return lax.ppermute(block, axis, route)]
    unnamed x56 -> x54, local copies, waits for them, and re-layouts: 14 us -> 13.9 us
  transfers between devices with their start and end apart: 11 -> 12, of which waited for: 6 -> 7; matrix products, arithmetic and copies ran while one was open for 8% -> 6% of each run, Pallas kernels for 0% -> 0%
where the time goes in v1:
time: 648 us; the launch traced here: 640 us
  waiting for transfers between devices  365 us (56%)
  local copies, waits for them, and re-layouts  119 us (18%)
  matrix products  103 us (16%)
  other arithmetic  21.9 us (3%)
  starting transfers between devices  16.3 us (3%)
  between operations  14.7 us (2%)
    psum x1, waiting for transfers between devices, local(): lax.psum(array_here, axis_name=net_axis)  202 us
    psum x1, waiting for transfers between devices, local(): lax.psum(lax.psum(array_here, axis_name=net_axis), axis_key)  128 us
    ppermute x10, waiting for transfers between devices, shifted_2(): return lax.ppermute(block, axis, route)  35.3 us
    concatenate x3, local copies, waits for them, and re-layouts, attend_back(): jnp.concatenate([grad_query.reshape(shape_out), grad_key.reshape(shape_ou...  24.6 us
    dot_general x1, matrix products, attend_back(): jnp.einsum('whqk,wqhd->wkhd', score_half, queries, preferred_element_type...  20.1 us
    dot_general x1, matrix products, attend_back(): jnp.einsum('whqk,wkhd->wqhd', score_half, keys_part, preferred_element_ty...  19.8 us
    ppermute x10, starting transfers between devices, shifted_2(): return lax.ppermute(block, axis, route)  16.3 us
    another operation x2, local copies, waits for them, and re-layouts, split_heads(): return tensor.reshape(tensor.shape[0], tensor.shape[1], HEADS, -1)  15.3 us
  transfers between devices with their start and end apart: 12, of which 7 were waited for; matrix products, arithmetic and copies ran while one was open for 6% of the time, Pallas kernels for 0%

profile of v1, /device:TPU:1, one launch (start us, length us, event | category | flops | bytes accessed | tf_op | source)
XLA Modules:
  0.0 639.5 jit_solution(6700651859739096700)
XLA Ops:
  7.2 0.9 convert_element_type.101
  8.1 4.7 collective-permute-start.2
  12.8 1.8 slice.88
  15.2 1.8 slice.73
  17.8 2.4 slice.72
  20.2 1.1 slice.87
  21.3 1.5 collective-permute-start.3
  22.9 2.8 collective-permute-done.3
  26.4 0.8 gt.22
  27.8 0.8 gt.24
  28.6 1.7 broadcast_or_fusion
  30.3 2.7 collective-permute-done
  32.9 1.0 pad_maximum_fusion.7
  33.9 1.9 collective-permute-start.1
  35.8 1.6 pad_maximum_fusion.6
  37.5 4.3 collective-permute-start.7
  41.7 1.4 slice_maximum_fusion.1
  43.2 2.8 slice_maximum_fusion
  48.6 1.7 pad_maximum_fusion.3
  50.3 1.2 copy-done.18
  51.6 1.4 convolution_convert_fusion.1
  53.0 1.3 copy.38
  55.5 4.5 convolution_convert_fusion
  60.5 2.3 fusion.40
  62.8 4.2 copy.18
  66.9 4.1 copy.17
  71.1 4.2 copy.15
  75.2 8.2 %reshape_reshape.22 = bf16[16,64,24,32]{3,2,1,0:T(8,128)(2,1)} reshape(bf16[2,8,8,8,768]{4,3,2,1,0:T(8,128)(2,1)} %bitcast.88) | data formatting | bytes 3145728 | tf_op jit(solution)/shard_map/reshape;reshape | solution.py:32
  83.4 7.1 %copy.23 = bf16[16,64,24,32]{1,3,2,0:T(8,128)(2,1)} copy(bf16[16,64,24,32]{3,2,1,0:T(8,128)(2,1)} %reshape_reshape.22) | data formatting | bytes 3145728 | tf_op jit(solution)/shard_map/reshape;reshape | solution.py:32
  90.5 9.2 %fusion.42 = f32[16,24,64,64]{2,3,1,0:T(8,128)} fusion(bf16[16,64,24,32]{1,3,2,0:T(8,128)(2,1)} %copy.23, bf16[16,64,24,32]{1,3,2,0:T(8,128)(2,1)} %bitcast.83), kind=kOutput, calls=%fused_computation.69 | convolution fusion | flops 100663296 | bytes 9437184 | tf_op jit(solution)/shard_map/wqhd,wkhd->whqk/dot_general | solution.py:67
  99.7 10.5 %fusion.41 = (f32[16,24,64]{2,1,0:T(8,128)}, f32[16,24,64,64]{2,3,1,0:T(8,128)}) fusion(pred[16,64,64]{1,2,0:T(8,128)(4,1)} %broadcast_or_fusion, bf16[16,64,24,32]{1,3,2,0:T(8,128)(2,1)} %bitcast.95, bf16[16,64,24,32]{1,3,2,0:T(8,128)(2,1)} %bitcast.93), kind=kOutput, calls=%fused_computation.68 | convolution fusion | flops 106954816 | bytes 9601024 | tf_op jit(solution)/shard_map/sub | solution.py:50
  110.2 19.8 %convert_bitcast_fusion.2 = bf16[16,64,24,32]{1,3,2,0:T(8,128)(2,1)} fusion(bf16[16,64,24,32]{1,3,2,0:T(8,128)(2,1)} %bitcast.94, f32[16,24,64,64]{2,3,1,0:T(8,128)} %fusion.42, f32[16,24,64,64]{2,3,1,0:T(8,128)} %get-tuple-element.14, f32[16,24,64]{2,1,0:T(8,128)} %get-tuple-element.13), kind=kOutput, calls=%fused_computation.24 | convolution fusion | flops 112484416 | bytes 15826944 | tf_op jit(solution)/shard_map/whqk,wkhd->wqhd/dot_general | solution.py:78
  129.9 20.1 %convert_bitcast_fusion.1 = bf16[16,64,24,32]{1,3,2,0:T(8,128)(2,1)} fusion(bf16[16,64,24,32]{1,3,2,0:T(8,128)(2,1)} %bitcast.96, f32[16,24,64,64]{2,3,1,0:T(8,128)} %fusion.42, f32[16,24,64,64]{2,3,1,0:T(8,128)} %get-tuple-element.14, f32[16,24,64]{2,1,0:T(8,128)} %get-tuple-element.13), kind=kOutput, calls=%fused_computation.23 | convolution fusion | flops 112484416 | bytes 15826944 | tf_op jit(solution)/shard_map/whqk,wqhd->wkhd/dot_general | solution.py:81
  150.0 10.7 %convert_bitcast_fusion = bf16[16,64,24,32]{1,3,2,0:T(8,128)(2,1)} fusion(bf16[16,64,24,32]{1,3,2,0:T(8,128)(2,1)} %copy.23, f32[16,24,64,64]{2,3,1,0:T(8,128)} %get-tuple-element.14, f32[16,24,64]{2,1,0:T(8,128)} %get-tuple-element.13), kind=kOutput, calls=%fused_computation.22 | convolution fusion | flops 104595456 | bytes 9535488 | tf_op jit(solution)/shard_map/whqk,wqhd->wkhd/dot_general | solution.py:71
  160.8 8.2 %convert_bitcast_fusion.3 = bf16[16,64,24,32]{1,3,2,0:T(8,128)(2,1)} fusion(bf16[16,64,24,32]{1,3,2,0:T(8,128)(2,1)S(1)} %bitcast.84, f32[16,24,64,64]{2,3,1,0:T(8,128)} %get-tuple-element.14, f32[16,24,64]{2,1,0:T(8,128)S(1)} %copy-done.25), kind=kOutput, calls=%fused_computation.26 | convolution fusion | flops 104595456 | bytes 9535488 | tf_op jit(solution)/shard_map/whqk,wkhd->wqhd/dot_general | solution.py:53
  168.9 6.9 %copy.20 = bf16[16,64,24,32]{3,2,1,0:T(8,128)(2,1)} copy(bf16[16,64,24,32]{1,3,2,0:T(8,128)(2,1)} %convert_bitcast_fusion.3) | data formatting | bytes 3145728 | tf_op jit(solution)/shard_map/convert_element_type | solution.py:55
  175.8 8.2 %reshape_reshape.19 = bf16[2,8,8,8,768]{4,3,2,1,0:T(8,128)(2,1)} reshape(bf16[16,64,24,32]{3,2,1,0:T(8,128)(2,1)} %copy.20) | data formatting | bytes 3145728 | tf_op jit(solution)/shard_map/reshape;reshape | solution.py:27
  184.1 1.7 copy.21
  185.8 1.1 copy-done.17
  186.9 2.9 fusion.44
  189.8 6.9 %copy.30 = bf16[16,64,24,32]{3,2,1,0:T(8,128)(2,1)} copy(bf16[16,64,24,32]{1,3,2,0:T(8,128)(2,1)} %convert_bitcast_fusion) | data formatting | bytes 3145728 | tf_op jit(solution)/shard_map/convert_element_type | solution.py:73
  196.7 8.2 %concatenate.50 = bf16[2,8,8,8,768]{4,3,2,1,0:T(8,128)(2,1)} reshape(bf16[16,64,24,32]{3,2,1,0:T(8,128)(2,1)} %copy.30) | data formatting | bytes 3145728 | tf_op jit(solution)/shard_map/concatenate | solution.py:85
  204.9 6.9 %copy.27 = bf16[16,64,24,32]{3,2,1,0:T(8,128)(2,1)} copy(bf16[16,64,24,32]{1,3,2,0:T(8,128)(2,1)} %convert_bitcast_fusion.1) | data formatting | bytes 3145728 | tf_op jit(solution)/shard_map/convert_element_type | solution.py:83
  211.8 8.2 %concatenate.49 = bf16[2,8,8,8,768]{4,3,2,1,0:T(8,128)(2,1)} reshape(bf16[16,64,24,32]{3,2,1,0:T(8,128)(2,1)} %copy.27) | data formatting | bytes 3145728 | tf_op jit(solution)/shard_map/concatenate | solution.py:85
  220.0 6.9 %copy.25 = bf16[16,64,24,32]{3,2,1,0:T(8,128)(2,1)} copy(bf16[16,64,24,32]{1,3,2,0:T(8,128)(2,1)} %convert_bitcast_fusion.2) | data formatting | bytes 3145728 | tf_op jit(solution)/shard_map/convert_element_type | solution.py:80
  226.9 8.2 %concatenate.48 = bf16[2,8,8,8,768]{4,3,2,1,0:T(8,128)(2,1)} reshape(bf16[16,64,24,32]{3,2,1,0:T(8,128)(2,1)} %copy.25) | data formatting | bytes 3145728 | tf_op jit(solution)/shard_map/concatenate | solution.py:85
  235.2 2.5 maximum_bitcast_fusion
  238.2 0.9 copy-done.3
  239.6 1.6 copy-done.11
  241.2 6.2 fusion.43
  247.5 201.6 %all-reduce.7.cloned.1.call-done = (f32[768,2304]{1,0:T(8,128)}, f32[768,768]{1,0:T(8,128)}) async-done(((f32[768,2304]{1,0:T(8,128)}, f32[768,768]{1,0:T(8,128)}), (f32[768,2304]{1,0:T(8,128)}, f32[768,768]{1,0:T(8,128)})) %all-reduce.7.cloned.1.call-update) | async-done | bytes 9437200 | tf_op jit(solution)/shard_map/psum | solution.py:159
  449.2 3.3 convolution_convert_fusion.2
  452.5 1.8 collective-permute-start.4
  454.4 6.1 fusion.39
  460.7 1.1 multiply_convert_fusion.2
  462.0 2.0 collective-permute-done.8
  464.2 0.9 collective-permute-start.9
  465.1 15.2 %collective-permute-done.5 = bf16[4,64,768]{2,1,0:T(8,128)(2,1)S(1)} collective-permute-done((bf16[4,64,768]{2,1,0:T(8,128)(2,1)S(1)}, bf16[4,64,768]{2,1,0:T(8,128)(2,1)S(1)}, u32[]{:S(2)}, u32[]{:S(2)}) %collective-permute-start.5) | collective-permute-done | bytes 393248 | tf_op jit(solution)/shard_map/ppermute | solution.py:16
  480.3 1.9 add_convert_fusion.1
  482.2 12.5 %collective-permute-done.9 = bf16[4,64,768]{2,1,0:T(8,128)(2,1)S(1)} collective-permute-done((bf16[4,64,768]{2,1,0:T(8,128)(2,1)S(1)}, bf16[4,64,768]{2,1,0:T(8,128)(2,1)S(1)}, u32[]{:S(2)}, u32[]{:S(2)}) %collective-permute-start.9) | collective-permute-done | bytes 393248 | tf_op jit(solution)/shard_map/ppermute | solution.py:16
  494.7 1.9 add_convert_fusion
  496.6 127.9 %all-reduce.5.cloned.1.call-done = (f32[768,2304]{1,0:T(8,128)}, f32[768,768]{1,0:T(8,128)}) async-done(((f32[768,2304]{1,0:T(8,128)}, f32[768,768]{1,0:T(8,128)}), (f32[768,2304]{1,0:T(8,128)}, f32[768,768]{1,0:T(8,128)})) %all-reduce.5.cloned.1.call-update) | async-done | bytes 9437200 | tf_op jit(solution)/shard_map/psum | solution.py:158
  624.5 6.6 %copy.44 = f32[768,2304]{1,0:T(8,128)} copy(f32[768,2304]{1,0:T(8,128)} %get-tuple-element.20) | data formatting | bytes 14155776
  631.1 1.4 copy.45
  (83 shorter events, 8.8 us)
Async XLA Ops:
  7.2 48.3 %copy-start = (bf16[768,2304]{1,0:T(8,128)(2,1)S(1)}, bf16[768,2304]{1,0:T(8,128)(2,1)}, u32[]{:S(2)}) copy-start(bf16[768,2304]{1,0:T(8,128)(2,1)} %param.8) | copy-start | bytes 10616836
  7.2 442.0 %all-reduce.7.cloned.1.call-start = ((), (), s32[]{:S(2)}) async-start(), calls=%async_computation.1 | async-start | bytes 18874368 | tf_op jit(solution)/shard_map/psum | solution.py:159
  7.2 13.0 %copy-start.9 = (bf16[16,64,768]{2,1,0:T(8,128)(2,1)S(1)}, bf16[16,64,768]{2,1,0:T(8,128)(2,1)}, u32[]{:S(2)}) copy-start(bf16[16,64,768]{2,1,0:T(8,128)(2,1)} %param.7) | copy-start | bytes 4718596
  8.1 13.2 %collective-permute-start.2 = (bf16[4,64]{1,0:T(4,128)(2,1)S(1)}, bf16[4,64]{1,0:T(4,128)(2,1)S(1)}, u32[]{:S(2)}, u32[]{:S(2)}) collective-permute-start(bf16[4,64]{1,0:T(4,128)(2,1)S(1)} %slice.99), channel_id=1, source_target_pairs={{1,0},{2,1},{3,2},{4,3},{5,4},{6,5},{7,6},{0,7},{9,8},{10,9},{11,1... | collective-permute-start | bytes 1544 | tf_op jit(solution)/shard_map/ppermute | solution.py:16
  14.5 21.3 %collective-permute-start.6 = (bf16[4,64,768]{2,1,0:T(8,128)(2,1)}, bf16[4,64,768]{2,1,0:T(8,128)(2,1)}, u32[]{:S(2)}, u32[]{:S(2)}) collective-permute-start(bf16[4,64,768]{2,1,0:T(8,128)(2,1)} %slice.88), channel_id=1, source_target_pairs={{1,0},{2,1},{3,2},{4,3},{5,4},{6,5},{7,6},{0,7},{9,8},{10,9},{11,1... | collective-permute-start | bytes 1179656 | tf_op jit(solution)/shard_map/ppermute | solution.py:16
  16.9 16.0 %collective-permute-start = (bf16[4,64,768]{2,1,0:T(8,128)(2,1)}, bf16[4,64,768]{2,1,0:T(8,128)(2,1)}, u32[]{:S(2)}, u32[]{:S(2)}) collective-permute-start(bf16[4,64,768]{2,1,0:T(8,128)(2,1)} %slice.73), channel_id=1, source_target_pairs={{1,0},{2,1},{3,2},{4,3},{5,4},{6,5},{7,6},{0,7},{9,8},{10,9},{11,1... | collective-permute-start | bytes 1179656 | tf_op jit(solution)/shard_map/ppermute | solution.py:16
  21.3 4.4 collective-permute-start.3
  28.6 13.1 %copy-start.7 = (bf16[12,64,768]{2,1,0:T(8,128)(2,1)S(1)}, bf16[12,64,768]{2,1,0:T(8,128)(2,1)}, u32[]{:S(2)}) copy-start(bf16[12,64,768]{2,1,0:T(8,128)(2,1)} %slice.72) | copy-start | bytes 3538948
  30.3 12.9 %copy-start.6 = (bf16[12,64,768]{2,1,0:T(8,128)(2,1)S(1)}, bf16[12,64,768]{2,1,0:T(8,128)(2,1)}, u32[]{:S(2)}) copy-start(bf16[12,64,768]{2,1,0:T(8,128)(2,1)} %slice.87) | copy-start | bytes 3538948
  33.9 12.1 %collective-permute-start.1 = (bf16[16,4,768]{2,1,0:T(4,128)(2,1)S(1)}, bf16[16,4,768]{2,1,0:T(4,128)(2,1)S(1)}, u32[]{:S(2)}, u32[]{:S(2)}) collective-permute-start(bf16[16,4,768]{2,1,0:T(4,128)(2,1)S(1)} %pad_maximum_fusion.7), channel_id=1, source_target_pairs={{8,0},{16,8},{24,16},{32,24},{40,32},{48,40},{56,48},{64,56},{72,6... | collective-permute-start | bytes 294920 | tf_op jit(solution)/shard_map/ppermute | solution.py:16
  37.5 11.2 %collective-permute-start.7 = (bf16[16,4,768]{2,1,0:T(4,128)(2,1)}, bf16[16,4,768]{2,1,0:T(4,128)(2,1)}, u32[]{:S(2)}, u32[]{:S(2)}) collective-permute-start(bf16[16,4,768]{2,1,0:T(4,128)(2,1)} %pad_maximum_fusion.6), channel_id=1, source_target_pairs={{8,0},{16,8},{24,16},{32,24},{40,32},{48,40},{56,48},{64,56},{72,6... | collective-permute-start | bytes 294920 | tf_op jit(solution)/shard_map/ppermute | solution.py:16
  43.2 4.1 copy-start.1
  46.0 0.6 copy-start.12
  48.6 2.9 copy-start.24
  50.3 1.2 copy-start.18
  53.0 2.0 copy-start.2
  53.0 2.0 copy-start.13
  53.0 2.0 copy-start.20
  53.0 2.0 copy-start.22
  150.0 10.7 %copy-start.5 = (bf16[16,64,768]{1,2,0:T(8,128)(2,1)S(1)}, bf16[16,64,768]{1,2,0:T(8,128)(2,1)}, u32[]{:S(2)}) copy-start(bf16[16,64,768]{1,2,0:T(8,128)(2,1)} %copy.15) | copy-start | bytes 4718596
  150.0 10.7 %copy-start.25 = (f32[16,24,64]{2,1,0:T(8,128)S(1)}, f32[16,24,64]{2,1,0:T(8,128)}, u32[]{:S(2)}) copy-start(f32[16,24,64]{2,1,0:T(8,128)} %get-tuple-element.13) | copy-start | bytes 294916
  184.1 2.8 copy-start.19
  185.7 1.1 copy-start.17
  237.7 1.4 copy-start.3
  237.7 1.4 copy-start.14
  239.1 2.1 copy-start.11
  247.4 377.0 %all-reduce.5.cloned.1.call-start = ((), (), s32[]{:S(2)}) async-start(), calls=%async_computation | async-start | bytes 18874368 | tf_op jit(solution)/shard_map/psum | solution.py:158
  449.2 5.2 copy-start.4
  449.2 5.2 copy-start.15
  449.2 5.2 copy-start.21
  449.2 5.2 copy-start.23
  452.5 8.0 %collective-permute-start.4 = (bf16[16,4,768]{2,1,0:T(4,128)(2,1)S(1)}, bf16[16,4,768]{2,1,0:T(4,128)(2,1)S(1)}, u32[]{:S(2)}, u32[]{:S(2)}) collective-permute-start(bf16[16,4,768]{2,1,0:T(4,128)(2,1)S(1)} %slice.104), channel_id=1, source_target_pairs={{120,0},{0,8},{8,16},{16,24},{24,32},{32,40},{40,48},{48,56},{56,6... | collective-permute-start | bytes 294920 | tf_op jit(solution)/shard_map/ppermute | solution.py:16
  460.6 19.7 %collective-permute-start.5 = (bf16[4,64,768]{2,1,0:T(8,128)(2,1)S(1)}, bf16[4,64,768]{2,1,0:T(8,128)(2,1)S(1)}, u32[]{:S(2)}, u32[]{:S(2)}) collective-permute-start(bf16[4,64,768]{2,1,0:T(8,128)(2,1)S(1)} %pad_maximum_fusion.5), channel_id=1, source_target_pairs={{7,0},{0,1},{1,2},{2,3},{3,4},{4,5},{5,6},{6,7},{15,8},{8,9},{9,10... | collective-permute-start | bytes 1179656 | tf_op jit(solution)/shard_map/ppermute | solution.py:16
  460.7 19.6 %copy-start.8 = (bf16[16,64,768]{2,1,0:T(8,128)(2,1)S(1)}, bf16[16,64,768]{2,1,0:T(8,128)(2,1)}, u32[]{:S(2)}) copy-start(bf16[16,64,768]{2,1,0:T(8,128)(2,1)} %param.5) | copy-start | bytes 4718596
  461.9 2.1 collective-permute-start.8
  464.0 30.7 %copy-start.10 = (bf16[16,64,768]{2,1,0:T(8,128)(2,1)S(1)}, bf16[16,64,768]{2,1,0:T(8,128)(2,1)}, u32[]{:S(2)}) copy-start(bf16[16,64,768]{2,1,0:T(8,128)(2,1)} %param.7) | copy-start | bytes 4718596
  464.2 30.5 %collective-permute-start.9 = (bf16[4,64,768]{2,1,0:T(8,128)(2,1)S(1)}, bf16[4,64,768]{2,1,0:T(8,128)(2,1)S(1)}, u32[]{:S(2)}, u32[]{:S(2)}) collective-permute-start(bf16[4,64,768]{2,1,0:T(8,128)(2,1)S(1)} %pad_maximum_fusion.4), channel_id=1, source_target_pairs={{7,0},{0,1},{1,2},{2,3},{3,4},{4,5},{5,6},{6,7},{15,8},{8,9},{9,10... | collective-permute-start | bytes 1179656 | tf_op jit(solution)/shard_map/ppermute | solution.py:16
  624.5 6.6 %copy-start.16 = (f32[768,768]{1,0:T(8,128)S(1)}, f32[768,768]{1,0:T(8,128)}, u32[]{:S(2)}) copy-start(f32[768,768]{1,0:T(8,128)} %get-tuple-element.21) | copy-start | bytes 7077892
Sparse Core Ops, SparseCore 0:
  247.6 201.5 all-reduce.6
  451.7 172.7 all-reduce.4
